TPU v7x, 32 devices: a whole 2x2x4 slice. The times are simulated.
32 devices in a mesh: row: 4 (over y, x), col: 8 (over z, core).
Axes of the slice: x: 2, y: 2, z: 4, core: 2. Of those that a mesh axis runs over, the one named last changes fastest.
Arguments:
- loads: float32 [4, 8, 1024, 8], P('row', 'col'), may hold values from -6 to 6
- schur: float32 [4, 8, 1024, 1024], P('row', 'col'), may hold values from -0.5 to 4.5, as said below
- factor: float32 [4, 8, 1024, 1024], P('row', 'col'), may hold values from -0.5 to 0.6, as said below
- coarse_inverse: float32 [1536, 1536], P(('row', 'col')), may hold values from -0.5 to 1.5, as said below
- elements: int32 [4, 8], P('row', 'col'), may hold values from 4096 to 16383
- west_map: int32 [4, 8, 256], P('row', 'col'), may hold values from 0 to 255, each once within a row
- south_map: int32 [4, 8, 256], P('row', 'col'), may hold values from 0 to 255, each once within a row
- prim_local: int32 [4, 8, 48], P('row', 'col'), may hold values from 0 to 1023
- prim_coarse: int32 [4, 8, 48], P('row', 'col'), may hold values from 0 to 1535
Outputs:
- solution: float32 [4, 8, 1024, 8], P('row', 'col')
- residual: float32 [4, 8, 1024, 8], P('row', 'col')
Inputs may be any that keep to these rules, and one draw needn't show every extreme that they name: `schur`: symmetric positive definite. `factor`: symmetric positive definite. `coarse_inverse`: symmetric positive definite. `west_map`: each subdomain's row is a permutation of 0 to 255. `south_map`: each subdomain's row is a permutation of 0 to 255. `prim_local`: values may repeat. `prim_coarse`: values may repeat, within a subdomain and between subdomains.
All inputs are finite; a program needn't handle non-finite values.
Results may differ from a plain program's by a relative error of at most 0.0001.
Values sent between devices are 32-bit elements; how exact they have to be, the bound alone decides.
A program may use at most 128 MiB of HBM per device.

v0:
```python
import jax
import jax.numpy as jnp
from jax import lax
from jax.sharding import PartitionSpec as P

ELEM_BASE = 4096
HIGHEST_PRECISION = lax.Precision.HIGHEST


def from_behind(x, axis, by):
    devices = lax.axis_size(axis)
    pairs = [(i, i + by) for i in range(devices) if 0 <= i + by < devices]
    return lax.ppermute(x, axis, pairs)


def product(matrix, vectors):
    return jnp.dot(matrix, vectors, precision=HIGHEST_PRECISION, preferred_element_type=jnp.float32)


def body(
    loads, schur, factor, coarse_inverse, elements, west_map, south_map, prim_local, prim_coarse
):
    schur_block = schur[0, 0]
    factor_block = factor[0, 0]
    local_loads = loads[0, 0]
    sweep_count = elements[0, 0] // ELEM_BASE
    west_order = west_map[0, 0]
    south_order = south_map[0, 0]
    primal_local = prim_local[0, 0]
    primal_coarse = prim_coarse[0, 0]
    unknowns = schur_block.shape[0]
    face_size = unknowns // 4
    column = lax.axis_index("col")
    grid_row = lax.axis_index("row")
    neighbour_flags = jnp.stack(
        [
            column > 0,
            column < lax.axis_size("col") - 1,
            grid_row > 0,
            grid_row < lax.axis_size("row") - 1,
        ]
    )
    weights = jnp.where(neighbour_flags[jnp.arange(unknowns) // face_size], 0.5, 1.0).astype(
        jnp.float32
    )[:, None]

    def assemble(values):
        west_face = values[:face_size]
        east_face = values[face_size : 2 * face_size]
        south_face = values[2 * face_size : 3 * face_size]
        north_face = values[3 * face_size :]
        from_west = from_behind(east_face, "col", 1)
        west_add = jnp.take(from_west, west_order, axis=0)
        west_back = jnp.zeros_like(west_face).at[west_order].set(west_face)
        from_east = from_behind(west_back, "col", -1)
        from_south = from_behind(north_face, "row", 1)
        south_add = jnp.take(from_south, south_order, axis=0)
        south_back = jnp.zeros_like(south_face).at[south_order].set(south_face)
        from_north = from_behind(south_back, "row", -1)
        return values + jnp.concatenate([west_add, from_east, south_add, from_north], axis=0)

    def weighted_sum(first, second):
        return jnp.sum(weights * first * second, axis=0)

    all_primal = lax.all_gather(primal_coarse, ("row", "col"), axis=0, tiled=True)
    right_side = assemble(local_loads)
    residual = right_side
    scaled = weights * residual
    local = product(factor_block, scaled)

    def sweep(turn, present):
        return present + product(factor_block, scaled - product(schur_block, present))

    local = lax.fori_loop(1, sweep_count, sweep, local)
    picked = jnp.take(scaled, primal_local, axis=0)
    columns = jnp.take(coarse_inverse, all_primal, axis=1)
    solved = product(columns, lax.all_gather(picked, ("row", "col"), axis=0, tiled=True))
    whole = lax.all_gather(solved, ("row", "col"), axis=0, tiled=True)
    precond = assemble(
        weights
        * (
            local
            + jnp.zeros_like(scaled).at[primal_local].add(jnp.take(whole, primal_coarse, axis=0))
        )
    )
    product_now = lax.psum(weighted_sum(residual, precond), ("row", "col"))
    image = assemble(product(schur_block, precond))
    alpha = product_now / lax.psum(weighted_sum(precond, image), ("row", "col"))
    solution = alpha * precond
    residual = residual - alpha * image
    return (solution[None, None], residual[None, None])


def solution(mesh):
    placed = (
        P("row", "col", None, None),
        P("row", "col", None, None),
        P("row", "col", None, None),
        P(("row", "col"), None),
        P("row", "col"),
        P("row", "col", None),
        P("row", "col", None),
        P("row", "col", None),
        P("row", "col", None),
    )
    return jax.shard_map(
        body,
        mesh=mesh,
        in_specs=placed,
        out_specs=(P("row", "col", None, None), P("row", "col", None, None)),
        check_vma=False,
    )
```

profile of v0, /device:TPU:0, one launch (start us, length us, event | category | flops | bytes accessed | tf_op | source)
XLA Modules:
  0.0 256.3 jit_solution(8718719181798448319)
XLA Ops:
  0.6 0.7 compare_select_fusion.3
  1.3 0.7 fusion.39
  2.2 1.2 scatter_custom_fusion
  3.5 1.3 collective-permute-start.1
  4.8 0.7 compare_select_fusion.2
  5.6 1.2 scatter_custom_fusion.1
  6.8 1.3 collective-permute-start.3
  8.3 5.5 %collective-permute-start.2 = (f32[256,8]{1,0:T(8,128)S(1)}, f32[256,8]{1,0:T(8,128)S(1)}, u32[]{:S(2)}, u32[]{:S(2)}) collective-permute-start(f32[256,8]{1,0:T(8,128)S(1)} %bitcast.105), channel_id=1, source_target_pairs={{0,8},{8,16},{16,24},{1,9},{9,17},{17,25},{2,10},{10,18},{18,26},{... | collective-permute-start | bytes 24584 | tf_op jit(solution)/shard_map/ppermute | solution.py:13
  13.9 2.8 %collective-permute-start = (f32[256,8]{1,0:T(8,128)S(1)}, f32[256,8]{1,0:T(8,128)S(1)}, u32[]{:S(2)}, u32[]{:S(2)}) collective-permute-start(f32[256,8]{1,0:T(8,128)S(1)} %bitcast.104), channel_id=1, source_target_pairs={{0,1},{1,2},{2,3},{3,4},{4,5},{5,6},{6,7},{8,9},{9,10},{10,11},{11... | collective-permute-start | bytes 24584 | tf_op jit(solution)/shard_map/ppermute | solution.py:13
  19.3 0.7 compare_and_fusion.2
  20.0 0.7 compare_select_fusion.5
  20.7 0.7 compare_and_fusion.1
  21.4 0.7 compare_select_fusion.4
  22.1 0.7 bitcast_dynamic-update-slice_fusion
  22.8 41.8 %all-reduce = s32[1536]{0:T(1024)S(1)} all-reduce(s32[1536]{0:T(1024)S(1)} %bitcast_dynamic-update-slice_fusion), channel_id=2, replica_groups=mesh['row'=4,'col'=8] {'row','col'}, use_global_device_ids=true, to_apply=%add | all-reduce | flops 1536 | bytes 12288 | tf_op jit(solution)/shard_map/all_gather | solution.py:65
  65.4 1.2 copy.96
  66.6 2.6 %gather_fusion = f32[1536,48]{1,0:T(8,128)S(1)} fusion(f32[48,1536]{0,1:T(8,128)S(1)} %copy.96, s32[2048]{0:T(1024)S(1)} %pad_clamp_fusion), kind=kCustom, calls=%fused_computation.6 | custom fusion | bytes 595968 | tf_op jit(solution)/shard_map/jit(_take)/gather | solution.py:76
  69.2 0.7 gather_fusion.3
  70.0 0.7 gather_fusion.2
  71.1 5.7 %convolution_bitcast_fusion.2 = f32[1024,8]{0,1:T(8,128)S(1)} fusion(f32[1,1,1024,8]{2,3,1,0:T(8,128)S(1)} %copy-done.1, f32[1,1,256,8]{2,3,1,0:T(8,128)S(1)} %bitcast.107, f32[1,1,256,8]{2,3,1,0:T(8,128)S(1)} %bitcast.102, f32[1,1,256,8]{2,3,1,0:T(8,128)S(1)} %bitcast.106, f32[1,1,256,8]{2,3,1,0:T(8,128)S(1)} %bitcast.103, f32[1024]{0:T(1024)S(1)} %bitcast.98, ...), kind=kOutput, calls=%fused_computation.20 | convolution fusion | flops 100704256 | bytes 4296704 | tf_op jit(solution)/shard_map/dot_general | solution.py:17
  76.8 19.1 %while.10 = (s32[]{:T(128)}, f32[1024,8]{0,1:T(8,128)S(1)}, s32[]{:T(128)}, f32[1024,1024]{1,0:T(8,128)}, f32[1024,8]{0,1:T(8,128)S(1)}, /*index=5*/f32[1024,1024]{1,0:T(8,128)}, s32[]{:T(128)}) while((s32[]{:T(128)}, f32[1024,8]{0,1:T(8,128)S(1)}, s32[]{:T(128)}, f32[1024,1024]{1,0:T(8,128)}, f32[1024,8]{0,1:T(8,128)S(1)}, ...), condition=%wide.region_3.5_spmd, body=%wide.region_2.4_spmd.sunk | while | flops 201342976 | bytes 25362536 | solution.py:74
  76.9 5.9 %convolution_subtract_fusion.2 = f32[1024,8]{0,1:T(8,128)S(1)} fusion(f32[1024,8]{0,1:T(8,128)S(1)} %get-tuple-element.125, f32[1024,1024]{1,0:T(8,128)} %get-tuple-element.124, f32[1024,8]{0,1:T(8,128)S(1)} %get-tuple-element.115), kind=kOutput, calls=%fused_computation.18.clone.1 | convolution fusion | flops 100671488 | bytes 4292608 | tf_op jit(solution)/shard_map/while/body/dot_general | solution.py:17
  82.8 3.6 %fusion.55 = f32[1024,8]{0,1:T(8,128)S(1)} fusion(f32[1024,8]{0,1:T(8,128)S(1)} %get-tuple-element.115, f32[1024,8]{0,1:T(8,128)S(1)} %convolution_subtract_fusion.2, f32[1024,1024]{1,0:T(8,128)S(1)} %copy-done), kind=kOutput, calls=%fused_computation.17.clone.1 | convolution fusion | flops 100671488 | bytes 4292608 | tf_op jit(solution)/shard_map/while/body/dot_general | solution.py:17
  86.4 5.9 %convolution_subtract_fusion.2 = f32[1024,8]{0,1:T(8,128)S(1)} fusion(f32[1024,8]{0,1:T(8,128)S(1)} %get-tuple-element.125, f32[1024,1024]{1,0:T(8,128)} %get-tuple-element.124, f32[1024,8]{0,1:T(8,128)S(1)} %get-tuple-element.115), kind=kOutput, calls=%fused_computation.18.clone.1 | convolution fusion | flops 100671488 | bytes 4292608 | tf_op jit(solution)/shard_map/while/body/dot_general | solution.py:17
  92.3 3.6 %fusion.55 = f32[1024,8]{0,1:T(8,128)S(1)} fusion(f32[1024,8]{0,1:T(8,128)S(1)} %get-tuple-element.115, f32[1024,8]{0,1:T(8,128)S(1)} %convolution_subtract_fusion.2, f32[1024,1024]{1,0:T(8,128)S(1)} %copy-done), kind=kOutput, calls=%fused_computation.17.clone.1 | convolution fusion | flops 100671488 | bytes 4292608 | tf_op jit(solution)/shard_map/while/body/dot_general | solution.py:17
  96.8 37.1 %all-gather.1 = f32[32,48,8]{1,2,0:T(8,128)S(1)} all-gather(f32[1,48,8]{1,2,0:T(8,128)S(1)} %copy.98), channel_id=1, replica_groups=mesh['row'=4,'col'=8] {'row','col'}, dimensions={0}, use_global_device_ids=true | all-gather | bytes 50688 | tf_op jit(solution)/shard_map/all_gather | solution.py:77
  134.7 38.6 %all-gather.2 = f32[32,48,8]{1,2,0:T(8,128)S(1)} all-gather(f32[1,48,8]{1,2,0:T(8,128)S(1)} %convolution_bitcast_fusion.3), channel_id=1, replica_groups=mesh['row'=4,'col'=8] {'row','col'}, dimensions={0}, use_global_device_ids=true | all-gather | bytes 50688 | tf_op jit(solution)/shard_map/all_gather | solution.py:78
  173.5 1.1 scatter_custom_fusion.2
  174.9 1.3 collective-permute-start.6
  176.1 2.2 collective-permute-start.4
  178.5 1.2 scatter_custom_fusion.4
  179.8 1.3 collective-permute-start.7
  181.2 1.2 scatter_custom_fusion.3
  182.5 1.5 collective-permute-start.5
  184.1 0.7 gather_fusion.5
  185.1 0.7 gather_fusion.4
  185.9 3.0 %collective-permute-done.7 = f32[256,8]{0,1:T(8,128)S(1)} collective-permute-done((f32[256,8]{0,1:T(8,128)S(1)}, f32[256,8]{0,1:T(8,128)S(1)}, u32[]{:S(2)}, u32[]{:S(2)}) %collective-permute-start.7) | collective-permute-done | bytes 8224 | tf_op jit(solution)/shard_map/ppermute | solution.py:13
  188.9 5.6 %convolution_bitcast_fusion.1 = f32[1024,8]{0,1:T(8,128)S(1)} fusion(f32[1024,8]{0,1:T(8,128)S(1)} %maximum_add_fusion.2, f32[1,1,1024,1024]{3,2,1,0:T(8,128)} %bitcast.95), kind=kOutput, calls=%fused_computation.19 | convolution fusion | flops 100663296 | bytes 4259840 | tf_op jit(solution)/shard_map/dot_general | solution.py:17
  194.6 5.9 %collective-permute-start.10 = (f32[256,8]{0,1:T(8,128)S(1)}, f32[256,8]{0,1:T(8,128)S(1)}, u32[]{:S(2)}, u32[]{:S(2)}) collective-permute-start(f32[256,8]{0,1:T(8,128)S(1)} %get-tuple-element.55), channel_id=1, source_target_pairs={{0,8},{8,16},{16,24},{1,9},{9,17},{17,25},{2,10},{10,18},{18,26},{... | collective-permute-start | bytes 24584 | tf_op jit(solution)/shard_map/ppermute | solution.py:13
  200.6 4.0 %collective-permute-start.8 = (f32[256,8]{0,1:T(8,128)S(1)}, f32[256,8]{0,1:T(8,128)S(1)}, u32[]{:S(2)}, u32[]{:S(2)}) collective-permute-start(f32[256,8]{0,1:T(8,128)S(1)} %get-tuple-element.53), channel_id=1, source_target_pairs={{0,1},{1,2},{2,3},{3,4},{4,5},{5,6},{6,7},{8,9},{9,10},{10,11},{11... | collective-permute-start | bytes 24584 | tf_op jit(solution)/shard_map/ppermute | solution.py:13
  204.7 1.2 scatter_custom_fusion.6
  206.0 1.3 collective-permute-start.11
  207.4 1.2 scatter_custom_fusion.5
  208.7 1.3 collective-permute-start.9
  210.1 0.7 gather_fusion.7
  211.0 0.7 gather_fusion.6
  212.5 43.1 %all-reduce.1 = (f32[8]{0:T(128)S(1)}, f32[8]{0:T(128)S(1)}) all-reduce(f32[8]{0:T(128)S(1)} %get-tuple-element.38, f32[8]{0:T(128)S(1)} %get-tuple-element.37), channel_id=1, replica_groups=mesh['row'=4,'col'=8] {'row','col'}, use_global_device_ids=true, to_apply=%region_8.10 | all-reduce | flops 16 | bytes 128 | tf_op jit(solution)/shard_map/psum | solution.py:86
  255.6 0.7 subtract_bitcast_fusion
  (76 shorter events, 8.0 us)
Async XLA Ops:
  0.6 70.3 %copy-start.1 = (f32[1,1,1024,8]{2,3,1,0:T(8,128)S(1)}, f32[1,1,1024,8]{2,3,1,0:T(8,128)}, u32[]{:S(2)}) copy-start(f32[1,1,1024,8]{2,3,1,0:T(8,128)} %param.13) | copy-start | bytes 98308
  3.5 67.4 %collective-permute-start.1 = (f32[256,8]{0,1:T(8,128)S(1)}, f32[256,8]{0,1:T(8,128)S(1)}, u32[]{:S(2)}, u32[]{:S(2)}) collective-permute-start(f32[256,8]{0,1:T(8,128)S(1)} %copy.91), channel_id=1, source_target_pairs={{1,0},{2,1},{3,2},{4,3},{5,4},{6,5},{7,6},{9,8},{10,9},{11,10},{12... | collective-permute-start | bytes 24584 | tf_op jit(solution)/shard_map/ppermute | solution.py:13
  6.8 64.0 %collective-permute-start.3 = (f32[256,8]{0,1:T(8,128)S(1)}, f32[256,8]{0,1:T(8,128)S(1)}, u32[]{:S(2)}, u32[]{:S(2)}) collective-permute-start(f32[256,8]{0,1:T(8,128)S(1)} %copy.95), channel_id=1, source_target_pairs={{8,0},{16,8},{24,16},{9,1},{17,9},{25,17},{10,2},{18,10},{26,18},{... | collective-permute-start | bytes 24584 | tf_op jit(solution)/shard_map/ppermute | solution.py:13
  8.3 61.0 %collective-permute-start.2 = (f32[256,8]{1,0:T(8,128)S(1)}, f32[256,8]{1,0:T(8,128)S(1)}, u32[]{:S(2)}, u32[]{:S(2)}) collective-permute-start(f32[256,8]{1,0:T(8,128)S(1)} %bitcast.105), channel_id=1, source_target_pairs={{0,8},{8,16},{16,24},{1,9},{9,17},{17,25},{2,10},{10,18},{18,26},{... | collective-permute-start | bytes 24584 | tf_op jit(solution)/shard_map/ppermute | solution.py:13
  13.9 56.1 %collective-permute-start = (f32[256,8]{1,0:T(8,128)S(1)}, f32[256,8]{1,0:T(8,128)S(1)}, u32[]{:S(2)}, u32[]{:S(2)}) collective-permute-start(f32[256,8]{1,0:T(8,128)S(1)} %bitcast.104), channel_id=1, source_target_pairs={{0,1},{1,2},{2,3},{3,4},{4,5},{5,6},{6,7},{8,9},{9,10},{10,11},{11... | collective-permute-start | bytes 24584 | tf_op jit(solution)/shard_map/ppermute | solution.py:13
  76.9 5.9 %copy-start = (f32[1024,1024]{1,0:T(8,128)S(1)}, f32[1024,1024]{1,0:T(8,128)}, u32[]{:S(2)}) copy-start(f32[1024,1024]{1,0:T(8,128)} %get-tuple-element.126) | copy-start | bytes 12582916 | tf_op jit(solution)/shard_map/while
  86.4 5.9 %copy-start = (f32[1024,1024]{1,0:T(8,128)S(1)}, f32[1024,1024]{1,0:T(8,128)}, u32[]{:S(2)}) copy-start(f32[1024,1024]{1,0:T(8,128)} %get-tuple-element.126) | copy-start | bytes 12582916 | tf_op jit(solution)/shard_map/while
  174.9 9.1 %collective-permute-start.6 = (f32[256,8]{0,1:T(8,128)S(1)}, f32[256,8]{0,1:T(8,128)S(1)}, u32[]{:S(2)}, u32[]{:S(2)}) collective-permute-start(f32[256,8]{0,1:T(8,128)S(1)} %get-tuple-element.59), channel_id=1, source_target_pairs={{0,8},{8,16},{16,24},{1,9},{9,17},{17,25},{2,10},{10,18},{18,26},{... | collective-permute-start | bytes 24584 | tf_op jit(solution)/shard_map/ppermute | solution.py:13
  176.1 8.8 %collective-permute-start.4 = (f32[256,8]{0,1:T(8,128)S(1)}, f32[256,8]{0,1:T(8,128)S(1)}, u32[]{:S(2)}, u32[]{:S(2)}) collective-permute-start(f32[256,8]{0,1:T(8,128)S(1)} %get-tuple-element.57), channel_id=1, source_target_pairs={{0,1},{1,2},{2,3},{3,4},{4,5},{5,6},{6,7},{8,9},{9,10},{10,11},{11... | collective-permute-start | bytes 24584 | tf_op jit(solution)/shard_map/ppermute | solution.py:13
  179.8 9.1 %collective-permute-start.7 = (f32[256,8]{0,1:T(8,128)S(1)}, f32[256,8]{0,1:T(8,128)S(1)}, u32[]{:S(2)}, u32[]{:S(2)}) collective-permute-start(f32[256,8]{0,1:T(8,128)S(1)} %copy.111), channel_id=1, source_target_pairs={{8,0},{16,8},{24,16},{9,1},{17,9},{25,17},{10,2},{18,10},{26,18},{... | collective-permute-start | bytes 24584 | tf_op jit(solution)/shard_map/ppermute | solution.py:13
  182.5 6.4 %collective-permute-start.5 = (f32[256,8]{0,1:T(8,128)S(1)}, f32[256,8]{0,1:T(8,128)S(1)}, u32[]{:S(2)}, u32[]{:S(2)}) collective-permute-start(f32[256,8]{0,1:T(8,128)S(1)} %copy.107), channel_id=1, source_target_pairs={{1,0},{2,1},{3,2},{4,3},{5,4},{6,5},{7,6},{9,8},{10,9},{11,10},{12... | collective-permute-start | bytes 24584 | tf_op jit(solution)/shard_map/ppermute | solution.py:13
  194.6 15.4 %collective-permute-start.10 = (f32[256,8]{0,1:T(8,128)S(1)}, f32[256,8]{0,1:T(8,128)S(1)}, u32[]{:S(2)}, u32[]{:S(2)}) collective-permute-start(f32[256,8]{0,1:T(8,128)S(1)} %get-tuple-element.55), channel_id=1, source_target_pairs={{0,8},{8,16},{16,24},{1,9},{9,17},{17,25},{2,10},{10,18},{18,26},{... | collective-permute-start | bytes 24584 | tf_op jit(solution)/shard_map/ppermute | solution.py:13
  200.6 10.4 %collective-permute-start.8 = (f32[256,8]{0,1:T(8,128)S(1)}, f32[256,8]{0,1:T(8,128)S(1)}, u32[]{:S(2)}, u32[]{:S(2)}) collective-permute-start(f32[256,8]{0,1:T(8,128)S(1)} %get-tuple-element.53), channel_id=1, source_target_pairs={{0,1},{1,2},{2,3},{3,4},{4,5},{5,6},{6,7},{8,9},{9,10},{10,11},{11... | collective-permute-start | bytes 24584 | tf_op jit(solution)/shard_map/ppermute | solution.py:13
  206.0 6.2 %collective-permute-start.11 = (f32[256,8]{0,1:T(8,128)S(1)}, f32[256,8]{0,1:T(8,128)S(1)}, u32[]{:S(2)}, u32[]{:S(2)}) collective-permute-start(f32[256,8]{0,1:T(8,128)S(1)} %copy.119), channel_id=1, source_target_pairs={{8,0},{16,8},{24,16},{9,1},{17,9},{25,17},{10,2},{18,10},{26,18},{... | collective-permute-start | bytes 24584 | tf_op jit(solution)/shard_map/ppermute | solution.py:13
  208.7 3.7 %collective-permute-start.9 = (f32[256,8]{0,1:T(8,128)S(1)}, f32[256,8]{0,1:T(8,128)S(1)}, u32[]{:S(2)}, u32[]{:S(2)}) collective-permute-start(f32[256,8]{0,1:T(8,128)S(1)} %copy.115), channel_id=1, source_target_pairs={{1,0},{2,1},{3,2},{4,3},{5,4},{6,5},{7,6},{9,8},{10,9},{11,10},{12... | collective-permute-start | bytes 24584 | tf_op jit(solution)/shard_map/ppermute | solution.py:13
where the time goes:
time: 257 us; the launch traced here: 256 us
  blocking collectives  161 us (63%)
  matrix products  30.9 us (12%)
  starting transfers between devices  29.8 us (12%)
  local copies, waits for them, and re-layouts  20.7 us (8%)
  other arithmetic  8.95 us (3%)
  waiting for transfers between devices  3.55 us (1%)
    psum x1, blocking collectives, body(): product_now = lax.psum(weighted_sum(residual, precond), ('row', 'col'))  43.1 us
    all_gather x1, blocking collectives, body(): lax.all_gather(primal_coarse, ('row', 'col'), axis=0, tiled=True)  41.8 us
    all_gather x1, blocking collectives, body(): whole = lax.all_gather(solved, ('row', 'col'), axis=0, tiled=True)  38.6 us
    all_gather x1, blocking collectives, body(): lax.all_gather(picked, ('row', 'col'), axis=0, tiled=True)  37.1 us
    dot_general x7, matrix products, product(): jnp.dot(matrix, vectors, precision=HIGHEST_PRECISION, preferred_element_t...  30.9 us
    ppermute x12, starting transfers between devices, from_behind(): return lax.ppermute(x, axis, pairs)  29.8 us
  transfers between devices with their start and end apart: 12, of which 3 were waited for; matrix products, arithmetic and copies ran while one was open for 9% of the time, Pallas kernels for 0%

commit v1 on v0

--- a/solution.py
+++ b/solution.py
@@ -83,7 +83,9 @@
             + jnp.zeros_like(scaled).at[primal_local].add(jnp.take(whole, primal_coarse, axis=0))
         )
     )
-    product_now = lax.psum(weighted_sum(residual, precond), ("row", "col"))
+    product_now = weighted_sum(residual, precond)
+    for mesh_axis in ("col", "row"):
+        product_now = lax.psum(product_now, mesh_axis)
     image = assemble(product(schur_block, precond))
     alpha = product_now / lax.psum(weighted_sum(precond, image), ("row", "col"))
     solution = alpha * precond

time: 257 us -> 281 us (1.093)
  blocking collectives: 161 us -> 184 us
    psum x1 -> x3, blocking collectives: 43.1 us -> 66.4 us  [the longest x1 39.3 us: body(): alpha = product_now / lax.psum(weighted_sum(precond, image), ('row', 'col'))]
  transfers between devices with their start and end apart: 12 -> 12, of which waited for: 3 -> 3; matrix products, arithmetic and copies ran while one was open for 9% -> 8% of each run, Pallas kernels for 0% -> 0%
where the time goes in v1:
time: 281 us; the launch traced here: 280 us
  blocking collectives  184 us (65%)
  matrix products  30.9 us (11%)
  starting transfers between devices  29.8 us (11%)
  local copies, waits for them, and re-layouts  20.7 us (7%)
  other arithmetic  8.95 us (3%)
  waiting for transfers between devices  3.55 us (1%)
    all_gather x1, blocking collectives, body(): lax.all_gather(primal_coarse, ('row', 'col'), axis=0, tiled=True)  41.8 us
    psum x1, blocking collectives, body(): alpha = product_now / lax.psum(weighted_sum(precond, image), ('row', 'col'))  39.3 us
    all_gather x1, blocking collectives, body(): whole = lax.all_gather(solved, ('row', 'col'), axis=0, tiled=True)  38.6 us
    all_gather x1, blocking collectives, body(): lax.all_gather(picked, ('row', 'col'), axis=0, tiled=True)  37.1 us
    dot_general x7, matrix products, product(): jnp.dot(matrix, vectors, precision=HIGHEST_PRECISION, preferred_element_t...  30.9 us
    ppermute x12, starting transfers between devices, from_behind(): return lax.ppermute(x, axis, pairs)  29.8 us
    psum x2, blocking collectives, body(): product_now = lax.psum(product_now, mesh_axis)  27.1 us
  transfers between devices with their start and end apart: 12, of which 3 were waited for; matrix products, arithmetic and copies ran while one was open for 8% of the time, Pallas kernels for 0%

profile of v1, /device:TPU:0, one launch (start us, length us, event | category | flops | bytes accessed | tf_op | source)
XLA Modules:
  0.0 279.6 jit_solution(6947299285947438443)
XLA Ops:
  0.6 0.7 compare_select_fusion.3
  1.3 0.7 fusion.39
  2.2 1.2 scatter_custom_fusion
  3.5 1.3 collective-permute-start.1
  4.8 0.7 compare_select_fusion.2
  5.6 1.2 scatter_custom_fusion.1
  6.8 1.3 collective-permute-start.3
  8.3 5.5 %collective-permute-start.2 = (f32[256,8]{1,0:T(8,128)S(1)}, f32[256,8]{1,0:T(8,128)S(1)}, u32[]{:S(2)}, u32[]{:S(2)}) collective-permute-start(f32[256,8]{1,0:T(8,128)S(1)} %bitcast.105), channel_id=1, source_target_pairs={{0,8},{8,16},{16,24},{1,9},{9,17},{17,25},{2,10},{10,18},{18,26},{... | collective-permute-start | bytes 24584 | tf_op jit(solution)/shard_map/ppermute | solution.py:13
  13.9 2.8 collective-permute-start
  19.3 0.7 compare_and_fusion.2
  20.7 0.7 compare_and_fusion.1
  22.1 0.7 bitcast_dynamic-update-slice_fusion
  22.8 41.8 %all-reduce = s32[1536]{0:T(1024)S(1)} all-reduce(s32[1536]{0:T(1024)S(1)} %bitcast_dynamic-update-slice_fusion), channel_id=2, replica_groups=mesh['row'=4,'col'=8] {'row','col'}, use_global_device_ids=true, to_apply=%add | all-reduce | flops 1536 | bytes 12288 | tf_op jit(solution)/shard_map/all_gather | solution.py:65
  65.4 1.2 copy.96
  66.6 2.6 gather_fusion
  69.2 0.7 gather_fusion.3
  70.0 0.7 gather_fusion.2
  71.1 5.7 %convolution_bitcast_fusion.2 = f32[1024,8]{0,1:T(8,128)S(1)} fusion(f32[1,1,1024,8]{2,3,1,0:T(8,128)S(1)} %copy-done.1, f32[1,1,256,8]{2,3,1,0:T(8,128)S(1)} %bitcast.107, f32[1,1,256,8]{2,3,1,0:T(8,128)S(1)} %bitcast.102, f32[1,1,256,8]{2,3,1,0:T(8,128)S(1)} %bitcast.106, f32[1,1,256,8]{2,3,1,0:T(8,128)S(1)} %bitcast.103, f32[1024]{0:T(1024)S(1)} %bitcast.98, ...), kind=kOutput, calls=%fused_computation.20 | convolution fusion | flops 100704256 | bytes 4296704 | tf_op jit(solution)/shard_map/dot_general | solution.py:17
  76.8 19.1 %while.10 = (s32[]{:T(128)}, f32[1024,8]{0,1:T(8,128)S(1)}, s32[]{:T(128)}, f32[1024,1024]{1,0:T(8,128)}, f32[1024,8]{0,1:T(8,128)S(1)}, /*index=5*/f32[1024,1024]{1,0:T(8,128)}, s32[]{:T(128)}) while((s32[]{:T(128)}, f32[1024,8]{0,1:T(8,128)S(1)}, s32[]{:T(128)}, f32[1024,1024]{1,0:T(8,128)}, f32[1024,8]{0,1:T(8,128)S(1)}, ...), condition=%wide.region_3.5_spmd, body=%wide.region_2.4_spmd.sunk | while | flops 201342976 | bytes 25362536 | solution.py:74
  76.9 5.9 %convolution_subtract_fusion.2 = f32[1024,8]{0,1:T(8,128)S(1)} fusion(f32[1024,8]{0,1:T(8,128)S(1)} %get-tuple-element.123, f32[1024,1024]{1,0:T(8,128)} %get-tuple-element.122, f32[1024,8]{0,1:T(8,128)S(1)} %get-tuple-element.113), kind=kOutput, calls=%fused_computation.18.clone.1 | convolution fusion | flops 100671488 | bytes 4292608 | tf_op jit(solution)/shard_map/while/body/dot_general | solution.py:17
  82.8 3.6 %fusion.55 = f32[1024,8]{0,1:T(8,128)S(1)} fusion(f32[1024,8]{0,1:T(8,128)S(1)} %get-tuple-element.113, f32[1024,8]{0,1:T(8,128)S(1)} %convolution_subtract_fusion.2, f32[1024,1024]{1,0:T(8,128)S(1)} %copy-done), kind=kOutput, calls=%fused_computation.17.clone.1 | convolution fusion | flops 100671488 | bytes 4292608 | tf_op jit(solution)/shard_map/while/body/dot_general | solution.py:17
  86.4 5.9 %convolution_subtract_fusion.2 = f32[1024,8]{0,1:T(8,128)S(1)} fusion(f32[1024,8]{0,1:T(8,128)S(1)} %get-tuple-element.123, f32[1024,1024]{1,0:T(8,128)} %get-tuple-element.122, f32[1024,8]{0,1:T(8,128)S(1)} %get-tuple-element.113), kind=kOutput, calls=%fused_computation.18.clone.1 | convolution fusion | flops 100671488 | bytes 4292608 | tf_op jit(solution)/shard_map/while/body/dot_general | solution.py:17
  92.3 3.6 %fusion.55 = f32[1024,8]{0,1:T(8,128)S(1)} fusion(f32[1024,8]{0,1:T(8,128)S(1)} %get-tuple-element.113, f32[1024,8]{0,1:T(8,128)S(1)} %convolution_subtract_fusion.2, f32[1024,1024]{1,0:T(8,128)S(1)} %copy-done), kind=kOutput, calls=%fused_computation.17.clone.1 | convolution fusion | flops 100671488 | bytes 4292608 | tf_op jit(solution)/shard_map/while/body/dot_general | solution.py:17
  96.8 37.1 %all-gather.1 = f32[32,48,8]{1,2,0:T(8,128)S(1)} all-gather(f32[1,48,8]{1,2,0:T(8,128)S(1)} %copy.98), channel_id=1, replica_groups=mesh['row'=4,'col'=8] {'row','col'}, dimensions={0}, use_global_device_ids=true | all-gather | bytes 50688 | tf_op jit(solution)/shard_map/all_gather | solution.py:77
  134.7 38.6 %all-gather.2 = f32[32,48,8]{1,2,0:T(8,128)S(1)} all-gather(f32[1,48,8]{1,2,0:T(8,128)S(1)} %convolution_bitcast_fusion.3), channel_id=1, replica_groups=mesh['row'=4,'col'=8] {'row','col'}, dimensions={0}, use_global_device_ids=true | all-gather | bytes 50688 | tf_op jit(solution)/shard_map/all_gather | solution.py:78
  173.5 1.1 scatter_custom_fusion.2
  174.9 1.3 collective-permute-start.6
  176.1 2.2 collective-permute-start.4
  178.5 1.2 scatter_custom_fusion.4
  179.8 1.3 collective-permute-start.7
  181.2 1.2 scatter_custom_fusion.3
  182.5 1.5 collective-permute-start.5
  184.1 0.7 gather_fusion.5
  185.1 0.7 gather_fusion.4
  185.9 3.0 %collective-permute-done.7 = f32[256,8]{0,1:T(8,128)S(1)} collective-permute-done((f32[256,8]{0,1:T(8,128)S(1)}, f32[256,8]{0,1:T(8,128)S(1)}, u32[]{:S(2)}, u32[]{:S(2)}) %collective-permute-start.7) | collective-permute-done | bytes 8224 | tf_op jit(solution)/shard_map/ppermute | solution.py:13
  188.9 5.6 %convolution_bitcast_fusion.1 = f32[1024,8]{0,1:T(8,128)S(1)} fusion(f32[1024,8]{0,1:T(8,128)S(1)} %maximum_add_fusion.2, f32[1,1,1024,1024]{3,2,1,0:T(8,128)} %bitcast.95), kind=kOutput, calls=%fused_computation.19 | convolution fusion | flops 100663296 | bytes 4259840 | tf_op jit(solution)/shard_map/dot_general | solution.py:17
  194.6 5.9 %collective-permute-start.10 = (f32[256,8]{0,1:T(8,128)S(1)}, f32[256,8]{0,1:T(8,128)S(1)}, u32[]{:S(2)}, u32[]{:S(2)}) collective-permute-start(f32[256,8]{0,1:T(8,128)S(1)} %get-tuple-element.53), channel_id=1, source_target_pairs={{0,8},{8,16},{16,24},{1,9},{9,17},{17,25},{2,10},{10,18},{18,26},{... | collective-permute-start | bytes 24584 | tf_op jit(solution)/shard_map/ppermute | solution.py:13
  200.6 4.0 %collective-permute-start.8 = (f32[256,8]{0,1:T(8,128)S(1)}, f32[256,8]{0,1:T(8,128)S(1)}, u32[]{:S(2)}, u32[]{:S(2)}) collective-permute-start(f32[256,8]{0,1:T(8,128)S(1)} %get-tuple-element.51), channel_id=1, source_target_pairs={{0,1},{1,2},{2,3},{3,4},{4,5},{5,6},{6,7},{8,9},{9,10},{10,11},{11... | collective-permute-start | bytes 24584 | tf_op jit(solution)/shard_map/ppermute | solution.py:13
  204.7 1.2 scatter_custom_fusion.6
  206.0 1.3 collective-permute-start.11
  207.4 1.2 scatter_custom_fusion.5
  208.7 1.3 collective-permute-start.9
  210.1 0.7 gather_fusion.7
  211.0 0.7 gather_fusion.6
  212.5 16.0 %psum.21 = f32[8]{0:T(128)S(1)} all-reduce(f32[8]{0:T(128)S(1)} %get-tuple-element.38), channel_id=1, replica_groups=mesh['row'=4,'col'=8] {'col'}, use_global_device_ids=true, to_apply=%region_8.10 | all-reduce | flops 8 | bytes 64 | tf_op jit(solution)/shard_map/psum | solution.py:88
  228.5 39.3 %psum.23 = f32[8]{0:T(128)S(1)} all-reduce(f32[8]{0:T(128)S(1)} %get-tuple-element.37), channel_id=1, replica_groups=mesh['row'=4,'col'=8] {'row','col'}, use_global_device_ids=true, to_apply=%region_13.15 | all-reduce | flops 8 | bytes 64 | tf_op jit(solution)/shard_map/psum | solution.py:90
  267.8 11.2 %psum.22 = f32[8]{0:T(128)S(1)} all-reduce(f32[8]{0:T(128)S(1)} %psum.21), channel_id=1, replica_groups=mesh['row'=4,'col'=8] {'row'}, use_global_device_ids=true, to_apply=%region_9.11 | all-reduce | flops 8 | bytes 64 | tf_op jit(solution)/shard_map/psum | solution.py:88
  278.9 0.7 subtract_bitcast_fusion
  (78 shorter events, 9.3 us)
Async XLA Ops:
  0.6 70.3 %copy-start.1 = (f32[1,1,1024,8]{2,3,1,0:T(8,128)S(1)}, f32[1,1,1024,8]{2,3,1,0:T(8,128)}, u32[]{:S(2)}) copy-start(f32[1,1,1024,8]{2,3,1,0:T(8,128)} %param.13) | copy-start | bytes 98308
  3.5 67.4 %collective-permute-start.1 = (f32[256,8]{0,1:T(8,128)S(1)}, f32[256,8]{0,1:T(8,128)S(1)}, u32[]{:S(2)}, u32[]{:S(2)}) collective-permute-start(f32[256,8]{0,1:T(8,128)S(1)} %copy.91), channel_id=1, source_target_pairs={{1,0},{2,1},{3,2},{4,3},{5,4},{6,5},{7,6},{9,8},{10,9},{11,10},{12... | collective-permute-start | bytes 24584 | tf_op jit(solution)/shard_map/ppermute | solution.py:13
  6.8 64.0 %collective-permute-start.3 = (f32[256,8]{0,1:T(8,128)S(1)}, f32[256,8]{0,1:T(8,128)S(1)}, u32[]{:S(2)}, u32[]{:S(2)}) collective-permute-start(f32[256,8]{0,1:T(8,128)S(1)} %copy.95), channel_id=1, source_target_pairs={{8,0},{16,8},{24,16},{9,1},{17,9},{25,17},{10,2},{18,10},{26,18},{... | collective-permute-start | bytes 24584 | tf_op jit(solution)/shard_map/ppermute | solution.py:13
  8.3 61.0 %collective-permute-start.2 = (f32[256,8]{1,0:T(8,128)S(1)}, f32[256,8]{1,0:T(8,128)S(1)}, u32[]{:S(2)}, u32[]{:S(2)}) collective-permute-start(f32[256,8]{1,0:T(8,128)S(1)} %bitcast.105), channel_id=1, source_target_pairs={{0,8},{8,16},{16,24},{1,9},{9,17},{17,25},{2,10},{10,18},{18,26},{... | collective-permute-start | bytes 24584 | tf_op jit(solution)/shard_map/ppermute | solution.py:13
  13.9 56.1 %collective-permute-start = (f32[256,8]{1,0:T(8,128)S(1)}, f32[256,8]{1,0:T(8,128)S(1)}, u32[]{:S(2)}, u32[]{:S(2)}) collective-permute-start(f32[256,8]{1,0:T(8,128)S(1)} %bitcast.104), channel_id=1, source_target_pairs={{0,1},{1,2},{2,3},{3,4},{4,5},{5,6},{6,7},{8,9},{9,10},{10,11},{11... | collective-permute-start | bytes 24584 | tf_op jit(solution)/shard_map/ppermute | solution.py:13
  76.9 5.9 %copy-start = (f32[1024,1024]{1,0:T(8,128)S(1)}, f32[1024,1024]{1,0:T(8,128)}, u32[]{:S(2)}) copy-start(f32[1024,1024]{1,0:T(8,128)} %get-tuple-element.124) | copy-start | bytes 12582916 | tf_op jit(solution)/shard_map/while
  86.4 5.9 %copy-start = (f32[1024,1024]{1,0:T(8,128)S(1)}, f32[1024,1024]{1,0:T(8,128)}, u32[]{:S(2)}) copy-start(f32[1024,1024]{1,0:T(8,128)} %get-tuple-element.124) | copy-start | bytes 12582916 | tf_op jit(solution)/shard_map/while
  174.9 9.1 %collective-permute-start.6 = (f32[256,8]{0,1:T(8,128)S(1)}, f32[256,8]{0,1:T(8,128)S(1)}, u32[]{:S(2)}, u32[]{:S(2)}) collective-permute-start(f32[256,8]{0,1:T(8,128)S(1)} %get-tuple-element.57), channel_id=1, source_target_pairs={{0,8},{8,16},{16,24},{1,9},{9,17},{17,25},{2,10},{10,18},{18,26},{... | collective-permute-start | bytes 24584 | tf_op jit(solution)/shard_map/ppermute | solution.py:13
  176.1 8.8 %collective-permute-start.4 = (f32[256,8]{0,1:T(8,128)S(1)}, f32[256,8]{0,1:T(8,128)S(1)}, u32[]{:S(2)}, u32[]{:S(2)}) collective-permute-start(f32[256,8]{0,1:T(8,128)S(1)} %get-tuple-element.55), channel_id=1, source_target_pairs={{0,1},{1,2},{2,3},{3,4},{4,5},{5,6},{6,7},{8,9},{9,10},{10,11},{11... | collective-permute-start | bytes 24584 | tf_op jit(solution)/shard_map/ppermute | solution.py:13
  179.8 9.1 %collective-permute-start.7 = (f32[256,8]{0,1:T(8,128)S(1)}, f32[256,8]{0,1:T(8,128)S(1)}, u32[]{:S(2)}, u32[]{:S(2)}) collective-permute-start(f32[256,8]{0,1:T(8,128)S(1)} %copy.111), channel_id=1, source_target_pairs={{8,0},{16,8},{24,16},{9,1},{17,9},{25,17},{10,2},{18,10},{26,18},{... | collective-permute-start | bytes 24584 | tf_op jit(solution)/shard_map/ppermute | solution.py:13
  182.5 6.4 %collective-permute-start.5 = (f32[256,8]{0,1:T(8,128)S(1)}, f32[256,8]{0,1:T(8,128)S(1)}, u32[]{:S(2)}, u32[]{:S(2)}) collective-permute-start(f32[256,8]{0,1:T(8,128)S(1)} %copy.107), channel_id=1, source_target_pairs={{1,0},{2,1},{3,2},{4,3},{5,4},{6,5},{7,6},{9,8},{10,9},{11,10},{12... | collective-permute-start | bytes 24584 | tf_op jit(solution)/shard_map/ppermute | solution.py:13
  194.6 15.4 %collective-permute-start.10 = (f32[256,8]{0,1:T(8,128)S(1)}, f32[256,8]{0,1:T(8,128)S(1)}, u32[]{:S(2)}, u32[]{:S(2)}) collective-permute-start(f32[256,8]{0,1:T(8,128)S(1)} %get-tuple-element.53), channel_id=1, source_target_pairs={{0,8},{8,16},{16,24},{1,9},{9,17},{17,25},{2,10},{10,18},{18,26},{... | collective-permute-start | bytes 24584 | tf_op jit(solution)/shard_map/ppermute | solution.py:13
  200.6 10.4 %collective-permute-start.8 = (f32[256,8]{0,1:T(8,128)S(1)}, f32[256,8]{0,1:T(8,128)S(1)}, u32[]{:S(2)}, u32[]{:S(2)}) collective-permute-start(f32[256,8]{0,1:T(8,128)S(1)} %get-tuple-element.51), channel_id=1, source_target_pairs={{0,1},{1,2},{2,3},{3,4},{4,5},{5,6},{6,7},{8,9},{9,10},{10,11},{11... | collective-permute-start | bytes 24584 | tf_op jit(solution)/shard_map/ppermute | solution.py:13
  206.0 6.2 %collective-permute-start.11 = (f32[256,8]{0,1:T(8,128)S(1)}, f32[256,8]{0,1:T(8,128)S(1)}, u32[]{:S(2)}, u32[]{:S(2)}) collective-permute-start(f32[256,8]{0,1:T(8,128)S(1)} %copy.119), channel_id=1, source_target_pairs={{8,0},{16,8},{24,16},{9,1},{17,9},{25,17},{10,2},{18,10},{26,18},{... | collective-permute-start | bytes 24584 | tf_op jit(solution)/shard_map/ppermute | solution.py:13
  208.7 3.7 %collective-permute-start.9 = (f32[256,8]{0,1:T(8,128)S(1)}, f32[256,8]{0,1:T(8,128)S(1)}, u32[]{:S(2)}, u32[]{:S(2)}) collective-permute-start(f32[256,8]{0,1:T(8,128)S(1)} %copy.115), channel_id=1, source_target_pairs={{1,0},{2,1},{3,2},{4,3},{5,4},{6,5},{7,6},{9,8},{10,9},{11,10},{12... | collective-permute-start | bytes 24584 | tf_op jit(solution)/shard_map/ppermute | solution.py:13
